TPU v7x, 32 devices: a whole 2x2x4 slice. The times are simulated.
32 devices in a mesh: grp: 2 (over y), tile: 4 (over z), tm: 2 (over x), ch: 2 (over core).
Axes of the slice: x: 2, y: 2, z: 4, core: 2. Of those that a mesh axis runs over, the one named last changes fastest.
Arguments:
- latent: bfloat16 [8, 8, 64, 512], P(('grp', 'tm'), None, 'tile', 'ch'), parts along dimension 0, may hold values from -340 to 340
- norm_gain: float32 [512], P('ch'), may hold values from 0.1 to 1.9
- norm_shift: float32 [512], P('ch'), may hold values from -3 to 3
- kernel: bfloat16 [3, 3, 3, 512, 512], P(None, None, None, ('ch', 'tile', 'tm')), may hold values from -0.0546875 to 0.0546875
- conv_bias: float32 [512], P('ch'), may hold values from -3 to 3
- blend_profile: int32 [4], replicated, may hold values from 0 to 3
Outputs:
- decoded: bfloat16 [8, 8, 64, 512], P(('grp', 'tm'), None, 'tile', 'ch'), parts along dimension 0
There are 2 independent parts, one for each index of `grp`. A program takes and returns all parts, laid end to end along the dimension named above; an argument that names none is the same for every part. Nothing has to cross between parts.
All inputs are finite; a program needn't handle non-finite values.
Results may differ from a plain program's by a relative error of at most 0.0038.
The roundings to bfloat16 on the way count: a program that leaves them out, or rounds other values in their place, can miss the bound.
Values may be sent and summed in bfloat16 or wider, within the bound.
A program may use at most 64 MiB of HBM per device.

v0:
```python
import jax
import jax.numpy as jnp
from jax import lax
from jax.sharding import PartitionSpec as P

GROUPS = 32
RIM = 4


def with_halo(shard, sides, width):
    for axis, dim in sides:
        size, length = (lax.axis_size(axis), shard.shape[dim])
        up = [(i, (i + 1) % size) for i in range(size - 1)]
        down = [(j, i) for i, j in up]
        last = lax.slice_in_dim(shard, length - width, length, axis=dim)
        leading = lax.slice_in_dim(shard, 0, width, axis=dim)
        before = lax.ppermute(last, axis, up)
        after = lax.ppermute(leading, axis, down)
        shard = jnp.concatenate([before, shard, after], axis=dim)
    return shard


def passed_along(block, axis, distance):
    devices = range(lax.axis_size(axis))
    route = [(i - distance, i) for i in devices if i - distance in devices]
    return lax.ppermute(block, axis, route)


def ramp_weight(profile, position, margin):
    fraction = (position.astype(jnp.float32) + 0.5) / (2.0 * margin)
    exponent = 1.0 + profile.astype(jnp.float32)
    near_part = jnp.power(1.0 - fraction, exponent)
    far_part = jnp.power(fraction, exponent)
    return near_part / (near_part + far_part)


def frame_stats(values, colmask, groups):
    frame_count, row_count, col_count, chan_count = values.shape
    grouped = values.reshape(frame_count, row_count, col_count, groups, chan_count // groups)
    weight = colmask.reshape(1, 1, col_count, 1, 1)
    counted = row_count * (chan_count // groups) * jnp.sum(colmask)
    center = jnp.sum(grouped * weight, axis=(1, 2, 4)) / counted
    spread = (grouped - center[:, None, None, :, None]) * weight
    inverse = lax.rsqrt(jnp.sum(spread * spread, axis=(1, 2, 4)) / counted + 1e-06)
    return (center, inverse)


def activate(values, center, inverse, norm_gain, norm_shift, colmask, timemask, groups):
    frame_count, row_count, col_count, chan_count = values.shape
    grouped = values.reshape(frame_count, row_count, col_count, groups, chan_count // groups)
    normed = (grouped - center[:, None, None, :, None]) * inverse[:, None, None, :, None]
    normed = normed.reshape(values.shape) * norm_gain + norm_shift
    masked = jax.nn.silu(normed) * colmask[None, None, :, None] * timemask[:, None, None, None]
    return masked.astype(jnp.bfloat16)


def conv_taps(padded, kernel_part, frame_count, row_count, col_count):
    in_width = kernel_part.shape[3]
    running = None
    for tap_time in range(3):
        for tap_row in range(3):
            for tap_col in range(3):
                window = padded[
                    tap_time : tap_time + frame_count,
                    tap_row : tap_row + row_count,
                    tap_col : tap_col + col_count,
                ]
                contrib = jnp.dot(
                    window.reshape(-1, in_width),
                    kernel_part[tap_time, tap_row, tap_col],
                    preferred_element_type=jnp.float32,
                )
                running = contrib if running is None else running + contrib
    return running


def on_device(latent, norm_gain, norm_shift, kernel, conv_bias, blend_profile):
    frame_count, row_count, core_cols, chan_half = latent.shape
    out_chans = kernel.shape[4]
    groups = GROUPS // lax.axis_size("ch")
    ncols = core_cols + 2 * RIM
    tile_pos = lax.axis_index("tile")
    tile_count = lax.axis_size("tile")
    window_in = with_halo(latent, (("tile", 2),), RIM)
    cached = passed_along(window_in, "tm", 1)
    frames = jnp.concatenate([cached, window_in], axis=0).astype(jnp.float32)
    column = tile_pos * core_cols - RIM + jnp.arange(ncols, dtype=jnp.int32)
    colmask = ((column >= 0) & (column < tile_count * core_cols)).astype(jnp.float32)
    started = (lax.axis_index("tm") > 0).astype(jnp.float32)
    timemask = jnp.concatenate(
        [jnp.ones((2,), jnp.float32) * started, jnp.ones((frame_count,), jnp.float32)]
    )
    center, inverse = frame_stats(frames, colmask, groups)
    activated = activate(frames, center, inverse, norm_gain, norm_shift, colmask, timemask, groups)
    inputs = (jnp.pad(activated, ((0, 0), (1, 1), (1, 1), (0, 0))),)
    widths = (ncols,)

    def accumulate(shard_rows):
        return tuple(
            (
                conv_taps(source, shard_rows, frame_count, row_count, width_cols)
                for source, width_cols in zip(inputs, widths)
            )
        )

    totals = accumulate(lax.all_gather(kernel, ("tile", "tm"), axis=3, tiled=True))
    shaped = [
        running.reshape(frame_count, row_count, width_cols, out_chans)
        for running, width_cols in zip(totals, widths)
    ]
    joined = shaped[0]
    summed = lax.psum_scatter(joined, "ch", scatter_dimension=3, tiled=True)
    tile_out = (summed + conv_bias).astype(jnp.bfloat16)
    extended = with_halo(tile_out, (("tile", 2),), RIM)
    own_out = tile_out[:, :, RIM : RIM + core_cols]
    left_nbr = extended[:, :, :RIM]
    right_nbr = extended[:, :, ncols + RIM :]
    own_profile = lax.dynamic_index_in_dim(blend_profile, tile_pos, 0, keepdims=False)
    prev_profile = lax.dynamic_index_in_dim(
        blend_profile, jnp.maximum(tile_pos - 1, 0), 0, keepdims=False
    )
    offsets = jnp.arange(RIM, dtype=jnp.int32)
    left_weight = jnp.where(tile_pos > 0, ramp_weight(prev_profile, offsets + RIM, RIM), 0.0)
    right_weight = jnp.where(tile_pos < tile_count - 1, ramp_weight(own_profile, offsets, RIM), 1.0)
    left_wide = left_weight[None, None, :, None]
    right_wide = right_weight[None, None, :, None]
    own_float = own_out.astype(jnp.float32)
    head_cols = own_float[:, :, :RIM] * (1.0 - left_wide) + left_nbr.astype(jnp.float32) * left_wide
    tail_cols = own_float[:, :, core_cols - RIM :] * right_wide + right_nbr.astype(jnp.float32) * (
        1.0 - right_wide
    )
    middle = own_float[:, :, RIM : core_cols - RIM]
    return jnp.concatenate([head_cols, middle, tail_cols], axis=2).astype(jnp.bfloat16)


def solution(mesh):
    in_specs = (
        P(("grp", "tm"), None, "tile", "ch"),
        P("ch"),
        P("ch"),
        P(None, None, None, ("ch", "tile", "tm"), None),
        P("ch"),
        P(),
    )
    out_specs = P(("grp", "tm"), None, "tile", "ch")
    return jax.shard_map(
        on_device, mesh=mesh, in_specs=in_specs, out_specs=out_specs, check_vma=False
    )
```

profile of v0, /device:TPU:0, one launch (start us, length us, event | category | flops | bytes accessed | tf_op | source)
XLA Modules:
  0.0 158.9 jit_solution(7346280072205576620)
XLA Ops:
  8.2 4.9 %collective-permute-start = (bf16[2,8,4,256]{3,2,1,0:T(4,128)(2,1)S(1)}, bf16[2,8,4,256]{3,2,1,0:T(4,128)(2,1)S(1)}, u32[]{:S(2)}, u32[]{:S(2)}) collective-permute-start(bf16[2,8,4,256]{3,2,1,0:T(4,128)(2,1)S(1)} %get-tuple-element.40), channel_id=1, source_target_pairs={{0,4},{4,8},{8,12},{1,5},{5,9},{9,13},{2,6},{6,10},{10,14},{3,7},{... | collective-permute-start | bytes 98312 | tf_op jit(solution)/shard_map/ppermute | solution.py:17
  13.2 1.3 collective-permute-start.1
  14.7 4.2 %collective-permute-done.1 = bf16[2,8,4,256]{3,2,1,0:T(4,128)(2,1)S(1)} collective-permute-done((bf16[2,8,4,256]{3,2,1,0:T(4,128)(2,1)S(1)}, bf16[2,8,4,256]{3,2,1,0:T(4,128)(2,1)S(1)}, u32[]{:S(2)}, u32[]{:S(2)}) %collective-permute-start.1) | collective-permute-done | bytes 32800 | tf_op jit(solution)/shard_map/ppermute | solution.py:18
  19.0 1.0 pad_maximum_fusion.1
  20.0 3.4 %collective-permute-start.2 = (bf16[2,8,24,256]{3,2,1,0:T(8,128)(2,1)S(1)}, bf16[2,8,24,256]{3,2,1,0:T(8,128)(2,1)S(1)}, u32[]{:S(2)}, u32[]{:S(2)}) collective-permute-start(bf16[2,8,24,256]{3,2,1,0:T(8,128)(2,1)S(1)} %pad_maximum_fusion.1), channel_id=1, source_target_pairs={{0,2},{1,3},{4,6},{5,7},{8,10},{9,11},{12,14},{13,15},{16,18},{17,... | collective-permute-start | bytes 589832 | tf_op jit(solution)/shard_map/ppermute | solution.py:26
  25.2 1.1 concatenate.24
  26.3 5.6 %collective-permute-done.2 = bf16[2,8,24,256]{3,2,1,0:T(8,128)(2,1)S(1)} collective-permute-done((bf16[2,8,24,256]{3,2,1,0:T(8,128)(2,1)S(1)}, bf16[2,8,24,256]{3,2,1,0:T(8,128)(2,1)S(1)}, u32[]{:S(2)}, u32[]{:S(2)}) %collective-permute-start.2) | collective-permute-done | bytes 196640 | tf_op jit(solution)/shard_map/ppermute | solution.py:26
  31.9 1.1 concatenate.23
  32.9 1.2 fusion
  34.2 1.7 %fusion.3 = f32[4,16]{1,0:T(4,128)S(1)} fusion(f32[4,16]{1,0:T(4,128)S(1)} %broadcast_divide_fusion, f32[24]{0:T(128)S(1)} %and_convert_fusion, bf16[2,8,24,16,16]{4,3,2,1,0:T(8,128)(2,1)S(1)} %concatenate.24, bf16[2,8,24,16,16]{4,3,2,1,0:T(8,128)(2,1)S(1)} %concatenate.23), kind=kLoop, calls=%fused_computation.5 | loop fusion | flops 1179584 | bytes 393824 | tf_op jit(solution)/shard_map/reduce_sum | solution.py:44
  36.2 1.1 multiply_convert_fusion
  37.3 1.1 pad_slice_fusion
  38.4 1.3 pad_slice_fusion.1
  39.7 81.3 %all-gather.2.cloned.1.call-done = bf16[3,3,3,256,512]{4,3,2,1,0:T(8,128)(2,1)} async-done(((bf16[3,3,3,32,512]{4,3,2,1,0:T(8,128)(2,1)}), bf16[3,3,3,256,512]{4,3,2,1,0:T(8,128)(2,1)}) %all-gather.2.cloned.1.call-update) | async-done | bytes 7077904 | tf_op jit(solution)/shard_map/all_gather | solution.py:106
  121.1 1.4 fusion.4
  122.5 1.9 %convolution_add_fusion.25 = f32[384,512]{1,0:T(8,128)S(1)} fusion(f32[384,512]{1,0:T(8,128)S(1)} %fusion.4, bf16[384,256]{1,0:T(8,128)(2,1)} %bitcast.161, bf16[3,3,3,256,512]{4,3,2,1,0:T(8,128)(2,1)} %all-gather.2.cloned.1.call-done), kind=kOutput, calls=%fused_computation.56 | convolution fusion | flops 100859904 | bytes 2031616 | tf_op jit(solution)/shard_map/dot_general | solution.py:68
  124.5 1.2 convolution_add_fusion.24
  125.7 1.2 convolution_add_fusion.23
  132.9 1.1 convolution_add_fusion
  136.1 4.6 %reduce-scatter.2.cloned.1.call-done = f32[2,8,24,256]{3,2,1,0:T(8,128)} async-done(((f32[2,8,24,512]{3,2,1,0:T(8,128)}), f32[2,8,24,256]{3,2,1,0:T(8,128)}) %reduce-scatter.2.cloned.1.call-update) | async-done | bytes 393232 | tf_op jit(solution)/shard_map/reduce_scatter | solution.py:112
  140.7 1.0 add_convert_fusion
  141.7 3.6 %collective-permute-start.3 = (bf16[2,8,4,256]{3,2,1,0:T(4,128)(2,1)S(1)}, bf16[2,8,4,256]{3,2,1,0:T(4,128)(2,1)S(1)}, u32[]{:S(2)}, u32[]{:S(2)}) collective-permute-start(bf16[2,8,4,256]{3,2,1,0:T(4,128)(2,1)S(1)} %get-tuple-element.38), channel_id=1, source_target_pairs={{0,4},{4,8},{8,12},{1,5},{5,9},{9,13},{2,6},{6,10},{10,14},{3,7},{... | collective-permute-start | bytes 98312 | tf_op jit(solution)/shard_map/ppermute | solution.py:17
  145.4 1.3 collective-permute-start.4
  146.9 4.2 %collective-permute-done.4 = bf16[2,8,4,256]{3,2,1,0:T(4,128)(2,1)S(1)} collective-permute-done((bf16[2,8,4,256]{3,2,1,0:T(4,128)(2,1)S(1)}, bf16[2,8,4,256]{3,2,1,0:T(4,128)(2,1)S(1)}, u32[]{:S(2)}, u32[]{:S(2)}) %collective-permute-start.4) | collective-permute-done | bytes 32800 | tf_op jit(solution)/shard_map/ppermute | solution.py:18
  (72 shorter events, 11.0 us)
Async XLA Ops:
  6.5 29.7 %copy-start.1 = (bf16[2,8,16,256]{3,2,1,0:T(8,128)(2,1)S(1)}, bf16[2,8,16,256]{3,2,1,0:T(8,128)(2,1)}, u32[]{:S(2)}) copy-start(bf16[2,8,16,256]{3,2,1,0:T(8,128)(2,1)} %param.6) | copy-start | bytes 393220
  6.5 29.7 %copy-start.11 = (f32[256]{0:T(256)S(1)}, f32[256]{0:T(256)}, u32[]{:S(2)}) copy-start(f32[256]{0:T(256)} %param.7) | copy-start | bytes 3076
  6.5 29.7 %copy-start.10 = (f32[256]{0:T(256)S(1)}, f32[256]{0:T(256)}, u32[]{:S(2)}) copy-start(f32[256]{0:T(256)} %param.8) | copy-start | bytes 3076
  6.5 114.5 %all-gather.2.cloned.1.call-start = ((), (), s32[]{:S(2)}) async-start(), calls=%async_computation.1 | async-start | bytes 7962624 | tf_op jit(solution)/shard_map/all_gather | solution.py:106
  7.3 133.4 %reduce-scatter.2.cloned.1.call-start = ((), (), s32[]{:S(2)}) async-start(), calls=%async_computation.2 | async-start | bytes 1179648 | tf_op jit(solution)/shard_map/reduce_scatter | solution.py:112
  8.2 6.5 %collective-permute-start = (bf16[2,8,4,256]{3,2,1,0:T(4,128)(2,1)S(1)}, bf16[2,8,4,256]{3,2,1,0:T(4,128)(2,1)S(1)}, u32[]{:S(2)}, u32[]{:S(2)}) collective-permute-start(bf16[2,8,4,256]{3,2,1,0:T(4,128)(2,1)S(1)} %get-tuple-element.40), channel_id=1, source_target_pairs={{0,4},{4,8},{8,12},{1,5},{5,9},{9,13},{2,6},{6,10},{10,14},{3,7},{... | collective-permute-start | bytes 98312 | tf_op jit(solution)/shard_map/ppermute | solution.py:17
  13.2 5.8 %collective-permute-start.1 = (bf16[2,8,4,256]{3,2,1,0:T(4,128)(2,1)S(1)}, bf16[2,8,4,256]{3,2,1,0:T(4,128)(2,1)S(1)}, u32[]{:S(2)}, u32[]{:S(2)}) collective-permute-start(bf16[2,8,4,256]{3,2,1,0:T(4,128)(2,1)S(1)} %get-tuple-element.41), channel_id=1, source_target_pairs={{4,0},{8,4},{12,8},{5,1},{9,5},{13,9},{6,2},{10,6},{14,10},{7,3},{... | collective-permute-start | bytes 98312 | tf_op jit(solution)/shard_map/ppermute | solution.py:18
  20.0 11.9 %collective-permute-start.2 = (bf16[2,8,24,256]{3,2,1,0:T(8,128)(2,1)S(1)}, bf16[2,8,24,256]{3,2,1,0:T(8,128)(2,1)S(1)}, u32[]{:S(2)}, u32[]{:S(2)}) collective-permute-start(bf16[2,8,24,256]{3,2,1,0:T(8,128)(2,1)S(1)} %pad_maximum_fusion.1), channel_id=1, source_target_pairs={{0,2},{1,3},{4,6},{5,7},{8,10},{9,11},{12,14},{13,15},{16,18},{17,... | collective-permute-start | bytes 589832 | tf_op jit(solution)/shard_map/ppermute | solution.py:26
  121.1 5.8 %copy-start = (bf16[3,3,3,256,512]{4,3,2,1,0:T(8,128)(2,1)S(1)}, bf16[3,3,3,256,512]{4,3,2,1,0:T(8,128)(2,1)}, u32[]{:S(2)}) copy-start(bf16[3,3,3,256,512]{4,3,2,1,0:T(8,128)(2,1)} %all-gather.2.cloned.1.call-done) | copy-start | bytes 21233668
  121.1 5.9 %copy-start.8 = (bf16[2,8,24,256]{3,2,1,0:T(8,128)(2,1)S(1)}, bf16[2,8,24,256]{3,2,1,0:T(8,128)(2,1)}, u32[]{:S(2)}) copy-start(bf16[2,8,24,256]{3,2,1,0:T(8,128)(2,1)} %get-tuple-element.34) | copy-start | bytes 589828
  127.5 1.9 %copy-start.7 = (bf16[2,8,24,256]{3,2,1,0:T(8,128)(2,1)S(1)}, bf16[2,8,24,256]{3,2,1,0:T(8,128)(2,1)}, u32[]{:S(2)}) copy-start(bf16[2,8,24,256]{3,2,1,0:T(8,128)(2,1)} %get-tuple-element.33) | copy-start | bytes 589828
  129.6 1.9 %copy-start.6 = (bf16[2,8,24,256]{3,2,1,0:T(8,128)(2,1)S(1)}, bf16[2,8,24,256]{3,2,1,0:T(8,128)(2,1)}, u32[]{:S(2)}) copy-start(bf16[2,8,24,256]{3,2,1,0:T(8,128)(2,1)} %get-tuple-element.29) | copy-start | bytes 589828
  129.9 1.9 %copy-start.5 = (bf16[2,8,24,256]{3,2,1,0:T(8,128)(2,1)S(1)}, bf16[2,8,24,256]{3,2,1,0:T(8,128)(2,1)}, u32[]{:S(2)}) copy-start(bf16[2,8,24,256]{3,2,1,0:T(8,128)(2,1)} %get-tuple-element.32) | copy-start | bytes 589828
  130.1 1.9 %copy-start.4 = (bf16[2,8,24,256]{3,2,1,0:T(8,128)(2,1)S(1)}, bf16[2,8,24,256]{3,2,1,0:T(8,128)(2,1)}, u32[]{:S(2)}) copy-start(bf16[2,8,24,256]{3,2,1,0:T(8,128)(2,1)} %get-tuple-element.30) | copy-start | bytes 589828
  130.4 1.9 %copy-start.3 = (bf16[2,8,24,256]{3,2,1,0:T(8,128)(2,1)S(1)}, bf16[2,8,24,256]{3,2,1,0:T(8,128)(2,1)}, u32[]{:S(2)}) copy-start(bf16[2,8,24,256]{3,2,1,0:T(8,128)(2,1)} %get-tuple-element.31) | copy-start | bytes 589828
  130.7 1.9 %copy-start.2 = (bf16[2,8,24,256]{3,2,1,0:T(8,128)(2,1)S(1)}, bf16[2,8,24,256]{3,2,1,0:T(8,128)(2,1)}, u32[]{:S(2)}) copy-start(bf16[2,8,24,256]{3,2,1,0:T(8,128)(2,1)} %get-tuple-element.28) | copy-start | bytes 589828
  131.2 2.8 %copy-start.9 = (s32[4]{0:T(128)S(1)}, s32[4]{0:T(128)}, u32[]{:S(2)}) copy-start(s32[4]{0:T(128)} %param.11) | copy-start | bytes 52
  131.2 9.4 %copy-start.12 = (f32[256]{0:T(256)S(1)}, f32[256]{0:T(256)}, u32[]{:S(2)}) copy-start(f32[256]{0:T(256)} %param.10) | copy-start | bytes 3076
  141.7 5.2 %collective-permute-start.3 = (bf16[2,8,4,256]{3,2,1,0:T(4,128)(2,1)S(1)}, bf16[2,8,4,256]{3,2,1,0:T(4,128)(2,1)S(1)}, u32[]{:S(2)}, u32[]{:S(2)}) collective-permute-start(bf16[2,8,4,256]{3,2,1,0:T(4,128)(2,1)S(1)} %get-tuple-element.38), channel_id=1, source_target_pairs={{0,4},{4,8},{8,12},{1,5},{5,9},{9,13},{2,6},{6,10},{10,14},{3,7},{... | collective-permute-start | bytes 98312 | tf_op jit(solution)/shard_map/ppermute | solution.py:17
  145.4 5.8 %collective-permute-start.4 = (bf16[2,8,4,256]{3,2,1,0:T(4,128)(2,1)S(1)}, bf16[2,8,4,256]{3,2,1,0:T(4,128)(2,1)S(1)}, u32[]{:S(2)}, u32[]{:S(2)}) collective-permute-start(bf16[2,8,4,256]{3,2,1,0:T(4,128)(2,1)S(1)} %get-tuple-element.39), channel_id=1, source_target_pairs={{4,0},{8,4},{12,8},{5,1},{9,5},{13,9},{6,2},{10,6},{14,10},{7,3},{... | collective-permute-start | bytes 98312 | tf_op jit(solution)/shard_map/ppermute | solution.py:18
Sparse Core Ops, SparseCore 0:
  9.5 111.4 all-gather.1
  134.2 6.4 reduce-scatter.1
where the time goes:
time: 159 us
  waiting for transfers between devices  101 us (64%)
  between operations  15.8 us (10%)
  starting transfers between devices  14.6 us (9%)
  matrix products  12.6 us (8%)
  other arithmetic  7.56 us (5%)
  local copies, waits for them, and re-layouts  7.04 us (4%)
    all_gather x1, waiting for transfers between devices, on_device(): lax.all_gather(kernel, ('tile', 'tm'), axis=3, tiled=True)  81.3 us
    dot_general x27, matrix products, conv_taps(): jnp.dot(window.reshape(-1, in_width), kernel_part[tap_time, tap_row, tap_...  12.6 us
    ppermute x2, starting transfers between devices, with_halo(): before = lax.ppermute(last, axis, up)  8.55 us
    ppermute x2, waiting for transfers between devices, with_halo(): after = lax.ppermute(leading, axis, down)  8.46 us
    ppermute x1, waiting for transfers between devices, passed_along(): return lax.ppermute(block, axis, route)  5.61 us
    reduce_scatter x1, waiting for transfers between devices, on_device(): summed = lax.psum_scatter(joined, 'ch', scatter_dimension=3, tiled=True)  4.61 us
    ppermute x1, starting transfers between devices, passed_along(): return lax.ppermute(block, axis, route)  3.41 us
  transfers between devices with their start and end apart: 7, of which 7 were waited for; matrix products, arithmetic and copies ran while one was open for 8% of the time, Pallas kernels for 0%

commit v1 on v0

--- a/solution.py
+++ b/solution.py
@@ -5,6 +5,27 @@
 
 GROUPS = 32
 RIM = 4
+
+
+def collect(x, axis, dim):
+    size, place, width = (lax.axis_size(axis), lax.axis_index(axis), x.shape[dim])
+    ahead = [(i, (i + 1) % size) for i in range(size)]
+    left = [(i, (i - 1) % size) for i in range(size)]
+    out = jnp.zeros((*x.shape[:dim], size * width, *x.shape[dim + 1 :]), x.dtype)
+    out = lax.dynamic_update_slice_in_dim(out, x, place * width, axis=dim)
+    from_left = from_right = x
+    half = size // 2
+    for hop in range(1, half + 1):
+        from_left = lax.ppermute(from_left, axis, ahead)
+        out = lax.dynamic_update_slice_in_dim(
+            out, from_left, (place - hop) % size * width, axis=dim
+        )
+        if hop < size - half:
+            from_right = lax.ppermute(from_right, axis, left)
+            out = lax.dynamic_update_slice_in_dim(
+                out, from_right, (place + hop) % size * width, axis=dim
+            )
+    return out
 
 
 def with_halo(shard, sides, width):
@@ -103,7 +124,7 @@
             )
         )
 
-    totals = accumulate(lax.all_gather(kernel, ("tile", "tm"), axis=3, tiled=True))
+    totals = accumulate(collect(kernel, ("tile", "tm"), 3))
     shaped = [
         running.reshape(frame_count, row_count, width_cols, out_chans)
         for running, width_cols in zip(totals, widths)

time: 159 us -> 219 us (1.38)
  matrix products: 12.6 us -> 34.1 us
  local copies, waits for them, and re-layouts: 7.04 us -> 23 us
  starting transfers between devices: 14.6 us -> 29.6 us
  waiting for transfers between devices: 101 us -> 107 us
    ppermute x0 -> x7, waiting for transfers between devices: none -> 85.8 us  [the longest x4 54.8 us: collect(): from_left = lax.ppermute(from_left, axis, ahead)]
    all_gather x1 -> x0, waiting for transfers between devices: 81.3 us -> none  [on_device(): lax.all_gather(kernel, ('tile', 'tm'), axis=3, tiled=True)]
    dot_general x27, matrix products: 12.6 us -> 34.1 us  [conv_taps(): jnp.dot(window.reshape(-1, in_width), kernel_part[tap_time, tap_row, tap_...]
    ppermute x0 -> x7, starting transfers between devices: none -> 19 us  [the longest x3 11.1 us: collect(): from_right = lax.ppermute(from_right, axis, left)]
    dynamic_update_slice x0 -> x8, local copies, waits for them, and re-layouts: none -> 14.3 us  [the longest x4 7.72 us: collect(): lax.dynamic_update_slice_in_dim(out, from_left, (place - hop) % size * wi...]
    ppermute x1, waiting for transfers between devices: 5.61 us -> 13.1 us  [passed_along(): return lax.ppermute(block, axis, route)]
    ppermute x2, waiting for transfers between devices: 8.46 us -> 4.23 us  [with_halo(): after = lax.ppermute(leading, axis, down)]
    broadcast_in_dim x0 -> x1, local copies, waits for them, and re-layouts: none -> 3.68 us  [collect(): out = jnp.zeros((*x.shape[:dim], size * width, *x.shape[dim + 1:]), x.dtype)]
  transfers between devices with their start and end apart: 7 -> 13, of which waited for: 7 -> 8; matrix products, arithmetic and copies ran while one was open for 8% -> 13% of each run, Pallas kernels for 0% -> 0%
where the time goes in v1:
time: 219 us; the launch traced here: 217 us
  waiting for transfers between devices  107 us (49%)
  matrix products  34.1 us (16%)
  starting transfers between devices  29.6 us (14%)
  local copies, waits for them, and re-layouts  23 us (11%)
  between operations  15.9 us (7%)
  other arithmetic  7.55 us (3%)
    ppermute x4, waiting for transfers between devices, collect(): from_left = lax.ppermute(from_left, axis, ahead)  54.8 us
    dot_general x27, matrix products, conv_taps(): jnp.dot(window.reshape(-1, in_width), kernel_part[tap_time, tap_row, tap_...  34.1 us
    ppermute x3, waiting for transfers between devices, collect(): from_right = lax.ppermute(from_right, axis, left)  31 us
    ppermute x1, waiting for transfers between devices, passed_along(): return lax.ppermute(block, axis, route)  13.1 us
    ppermute x3, starting transfers between devices, collect(): from_right = lax.ppermute(from_right, axis, left)  11.1 us
    ppermute x4, starting transfers between devices, collect(): from_left = lax.ppermute(from_left, axis, ahead)  7.9 us
    dynamic_update_slice x4, local copies, waits for them, and re-layouts, collect(): lax.dynamic_update_slice_in_dim(out, from_left, (place - hop) % size * wi...  7.72 us
    ppermute x2, starting transfers between devices, with_halo(): before = lax.ppermute(last, axis, up)  5.48 us
  transfers between devices with their start and end apart: 13, of which 8 were waited for; matrix products, arithmetic and copies ran while one was open for 13% of the time, Pallas kernels for 0%

profile of v1, /device:TPU:0, one launch (start us, length us, event | category | flops | bytes accessed | tf_op | source)
XLA Modules:
  0.0 217.3 jit_solution(3927187382463621431)
XLA Ops:
  6.5 2.9 %collective-permute-start.3 = (bf16[3,3,3,32,512]{4,3,2,1,0:T(8,128)(2,1)}, bf16[3,3,3,32,512]{4,3,2,1,0:T(8,128)(2,1)}, u32[]{:S(2)}, u32[]{:S(2)}) collective-permute-start(bf16[3,3,3,32,512]{4,3,2,1,0:T(8,128)(2,1)} %param.9), channel_id=1, source_target_pairs={{0,2},{2,4},{4,6},{6,8},{8,10},{10,12},{12,14},{14,0},{1,3},{3,5},... | collective-permute-start | bytes 2654216 | tf_op jit(solution)/shard_map/ppermute | solution.py:19
  9.5 3.0 %collective-permute-start.4 = (bf16[3,3,3,32,512]{4,3,2,1,0:T(8,128)(2,1)}, bf16[3,3,3,32,512]{4,3,2,1,0:T(8,128)(2,1)}, u32[]{:S(2)}, u32[]{:S(2)}) collective-permute-start(bf16[3,3,3,32,512]{4,3,2,1,0:T(8,128)(2,1)} %param.9), channel_id=1, source_target_pairs={{0,14},{2,0},{4,2},{6,4},{8,6},{10,8},{12,10},{14,12},{1,15},{3,1}... | collective-permute-start | bytes 2654216 | tf_op jit(solution)/shard_map/ppermute | solution.py:24
  13.4 1.9 collective-permute-start
  18.5 29.1 %collective-permute-done.3 = bf16[3,3,3,32,512]{4,3,2,1,0:T(8,128)(2,1)} collective-permute-done((bf16[3,3,3,32,512]{4,3,2,1,0:T(8,128)(2,1)}, bf16[3,3,3,32,512]{4,3,2,1,0:T(8,128)(2,1)}, u32[]{:S(2)}, u32[]{:S(2)}) %collective-permute-start.3) | collective-permute-done | bytes 884768 | tf_op jit(solution)/shard_map/ppermute | solution.py:19
  47.7 2.5 %collective-permute-start.5 = (bf16[3,3,3,32,512]{4,3,2,1,0:T(8,128)(2,1)}, bf16[3,3,3,32,512]{4,3,2,1,0:T(8,128)(2,1)}, u32[]{:S(2)}, u32[]{:S(2)}) collective-permute-start(bf16[3,3,3,32,512]{4,3,2,1,0:T(8,128)(2,1)} %collective-permute-done.3), channel_id=1, source_target_pairs={{0,2},{2,4},{4,6},{6,8},{8,10},{10,12},{12,14},{14,0},{1,3},{3,5},... | collective-permute-start | bytes 2654216 | tf_op jit(solution)/shard_map/ppermute | solution.py:19
  51.1 2.5 %collective-permute-start.2 = (bf16[2,8,24,256]{3,2,1,0:T(8,128)(2,1)S(1)}, bf16[2,8,24,256]{3,2,1,0:T(8,128)(2,1)S(1)}, u32[]{:S(2)}, u32[]{:S(2)}) collective-permute-start(bf16[2,8,24,256]{3,2,1,0:T(8,128)(2,1)S(1)} %pad_maximum_fusion.1), channel_id=1, source_target_pairs={{0,2},{1,3},{4,6},{5,7},{8,10},{9,11},{12,14},{13,15},{16,18},{17,... | collective-permute-start | bytes 589832 | tf_op jit(solution)/shard_map/ppermute | solution.py:47
  53.6 3.7 %broadcast_in_dim.6 = bf16[3,3,3,256,512]{4,3,2,1,0:T(8,128)(2,1)} broadcast(bf16[]{:T(256)} %constant.92.clone.1), dimensions={} | broadcast | bytes 7077890 | tf_op jit(solution)/shard_map/broadcast_in_dim | solution.py:14
  59.5 13.1 %collective-permute-done.2 = bf16[2,8,24,256]{3,2,1,0:T(8,128)(2,1)S(1)} collective-permute-done((bf16[2,8,24,256]{3,2,1,0:T(8,128)(2,1)S(1)}, bf16[2,8,24,256]{3,2,1,0:T(8,128)(2,1)S(1)}, u32[]{:S(2)}, u32[]{:S(2)}) %collective-permute-start.2) | collective-permute-done | bytes 196640 | tf_op jit(solution)/shard_map/ppermute | solution.py:47
  74.9 5.5 %collective-permute-start.6 = (bf16[3,3,3,32,512]{4,3,2,1,0:T(8,128)(2,1)}, bf16[3,3,3,32,512]{4,3,2,1,0:T(8,128)(2,1)}, u32[]{:S(2)}, u32[]{:S(2)}) collective-permute-start(bf16[3,3,3,32,512]{4,3,2,1,0:T(8,128)(2,1)} %collective-permute-done.4), channel_id=1, source_target_pairs={{0,14},{2,0},{4,2},{6,4},{8,6},{10,8},{12,10},{14,12},{1,15},{3,1}... | collective-permute-start | bytes 2654216 | tf_op jit(solution)/shard_map/ppermute | solution.py:24
  80.4 1.7 fusion.3
  83.6 30.9 %collective-permute-done.6 = bf16[3,3,3,32,512]{4,3,2,1,0:T(8,128)(2,1)} collective-permute-done((bf16[3,3,3,32,512]{4,3,2,1,0:T(8,128)(2,1)}, bf16[3,3,3,32,512]{4,3,2,1,0:T(8,128)(2,1)}, u32[]{:S(2)}, u32[]{:S(2)}) %collective-permute-start.6) | collective-permute-done | bytes 884768 | tf_op jit(solution)/shard_map/ppermute | solution.py:24
  114.5 2.6 %collective-permute-start.8 = (bf16[3,3,3,32,512]{4,3,2,1,0:T(8,128)(2,1)}, bf16[3,3,3,32,512]{4,3,2,1,0:T(8,128)(2,1)S(1)}, u32[]{:S(2)}, u32[]{:S(2)}) collective-permute-start(bf16[3,3,3,32,512]{4,3,2,1,0:T(8,128)(2,1)} %collective-permute-done.6), channel_id=1, source_target_pairs={{0,14},{2,0},{4,2},{6,4},{8,6},{10,8},{12,10},{14,12},{1,15},{3,1}... | collective-permute-start | bytes 2654216 | tf_op jit(solution)/shard_map/ppermute | solution.py:24
  117.2 16.4 %collective-permute-done.7 = bf16[3,3,3,32,512]{4,3,2,1,0:T(8,128)(2,1)} collective-permute-done((bf16[3,3,3,32,512]{4,3,2,1,0:T(8,128)(2,1)}, bf16[3,3,3,32,512]{4,3,2,1,0:T(8,128)(2,1)}, u32[]{:S(2)}, u32[]{:S(2)}) %collective-permute-start.7) | collective-permute-done | bytes 884768 | tf_op jit(solution)/shard_map/ppermute | solution.py:19
  133.6 2.5 %collective-permute-start.9 = (bf16[3,3,3,32,512]{4,3,2,1,0:T(8,128)(2,1)}, bf16[3,3,3,32,512]{4,3,2,1,0:T(8,128)(2,1)S(1)}, u32[]{:S(2)}, u32[]{:S(2)}) collective-permute-start(bf16[3,3,3,32,512]{4,3,2,1,0:T(8,128)(2,1)} %collective-permute-done.7), channel_id=1, source_target_pairs={{0,2},{2,4},{4,6},{6,8},{8,10},{10,12},{12,14},{14,0},{1,3},{3,5},... | collective-permute-start | bytes 2654216 | tf_op jit(solution)/shard_map/ppermute | solution.py:19
  136.5 2.3 %constant_dynamic-update-slice_fusion.6 = bf16[3,3,3,256,512]{4,3,2,1,0:T(8,128)(2,1)} fusion(bf16[3,3,3,256,512]{4,3,2,1,0:T(8,128)(2,1)} %constant_dynamic-update-slice_fusion.7, bf16[3,3,3,32,512]{4,3,2,1,0:T(8,128)(2,1)} %collective-permute-done.3, s32[]{:T(128)S(6)} %select_n.90), kind=kLoop, calls=%fused_computation.128 | loop fusion | bytes 1769476 | tf_op jit(solution)/shard_map/dynamic_update_slice | solution.py:20
  138.8 2.2 %constant_dynamic-update-slice_fusion.5 = bf16[3,3,3,256,512]{4,3,2,1,0:T(8,128)(2,1)} fusion(bf16[3,3,3,256,512]{4,3,2,1,0:T(8,128)(2,1)} %constant_dynamic-update-slice_fusion.6, bf16[3,3,3,32,512]{4,3,2,1,0:T(8,128)(2,1)} %collective-permute-done.4, s32[]{:T(128)S(6)} %select_n.92), kind=kLoop, calls=%fused_computation.127 | loop fusion | bytes 1769476 | tf_op jit(solution)/shard_map/dynamic_update_slice | solution.py:25
  141.0 2.2 %constant_dynamic-update-slice_fusion.4 = bf16[3,3,3,256,512]{4,3,2,1,0:T(8,128)(2,1)} fusion(bf16[3,3,3,256,512]{4,3,2,1,0:T(8,128)(2,1)} %constant_dynamic-update-slice_fusion.5, bf16[3,3,3,32,512]{4,3,2,1,0:T(8,128)(2,1)} %collective-permute-done.5, s32[]{:T(128)S(6)} %select_n.94), kind=kLoop, calls=%fused_computation.126 | loop fusion | bytes 1769476 | tf_op jit(solution)/shard_map/dynamic_update_slice | solution.py:20
  143.3 2.2 %constant_dynamic-update-slice_fusion.3 = bf16[3,3,3,256,512]{4,3,2,1,0:T(8,128)(2,1)} fusion(bf16[3,3,3,256,512]{4,3,2,1,0:T(8,128)(2,1)} %constant_dynamic-update-slice_fusion.4, bf16[3,3,3,32,512]{4,3,2,1,0:T(8,128)(2,1)} %collective-permute-done.6, s32[]{:T(128)S(6)} %select_n.96), kind=kLoop, calls=%fused_computation.125 | loop fusion | bytes 1769476 | tf_op jit(solution)/shard_map/dynamic_update_slice | solution.py:25
  145.5 2.2 %constant_dynamic-update-slice_fusion.2 = bf16[3,3,3,256,512]{4,3,2,1,0:T(8,128)(2,1)} fusion(bf16[3,3,3,256,512]{4,3,2,1,0:T(8,128)(2,1)} %constant_dynamic-update-slice_fusion.3, bf16[3,3,3,32,512]{4,3,2,1,0:T(8,128)(2,1)} %collective-permute-done.7, s32[]{:T(128)S(6)} %select_n.98), kind=kLoop, calls=%fused_computation.124 | loop fusion | bytes 1769476 | tf_op jit(solution)/shard_map/dynamic_update_slice | solution.py:20
  148.7 9.3 %collective-permute-done.9 = bf16[3,3,3,32,512]{4,3,2,1,0:T(8,128)(2,1)S(1)} collective-permute-done((bf16[3,3,3,32,512]{4,3,2,1,0:T(8,128)(2,1)}, bf16[3,3,3,32,512]{4,3,2,1,0:T(8,128)(2,1)S(1)}, u32[]{:S(2)}, u32[]{:S(2)}) %collective-permute-start.9) | collective-permute-done | bytes 884768 | tf_op jit(solution)/shard_map/ppermute | solution.py:19
  190.5 2.9 %fusion.28 = f32[384,512]{1,0:T(8,128)} fusion(f32[384,512]{1,0:T(8,128)S(1)} %fusion.29, f32[384,512]{1,0:T(8,128)S(1)} %fusion.30, f32[384,512]{1,0:T(8,128)S(1)} %fusion.31, f32[384,512]{1,0:T(8,128)S(1)} %fusion.32, f32[384,512]{1,0:T(8,128)S(1)} %fusion.33, f32[384,512]{1,0:T(8,128)S(1)} %fusion.34, f32[384,512]{1,0:T(8,128)S(1)} %fusion.35, ...), kind=kOutput, calls=%fused_computation.56 | convolution fusion | flops 105775104 | bytes 21692416 | tf_op jit(solution)/shard_map/dot_general | solution.py:89
  195.4 3.7 %reduce-scatter.2.cloned.1.call-done = f32[2,8,24,256]{3,2,1,0:T(8,128)} async-done(((f32[2,8,24,512]{3,2,1,0:T(8,128)}), f32[2,8,24,256]{3,2,1,0:T(8,128)}) %reduce-scatter.2.cloned.1.call-update) | async-done | bytes 393232 | tf_op jit(solution)/shard_map/reduce_scatter | solution.py:133
  200.2 3.6 %collective-permute-start.10 = (bf16[2,8,4,256]{3,2,1,0:T(4,128)(2,1)S(1)}, bf16[2,8,4,256]{3,2,1,0:T(4,128)(2,1)S(1)}, u32[]{:S(2)}, u32[]{:S(2)}) collective-permute-start(bf16[2,8,4,256]{3,2,1,0:T(4,128)(2,1)S(1)} %get-tuple-element.38), channel_id=1, source_target_pairs={{0,4},{4,8},{8,12},{1,5},{5,9},{9,13},{2,6},{6,10},{10,14},{3,7},{... | collective-permute-start | bytes 98312 | tf_op jit(solution)/shard_map/ppermute | solution.py:38
  205.3 4.2 %collective-permute-done.11 = bf16[2,8,4,256]{3,2,1,0:T(4,128)(2,1)S(1)} collective-permute-done((bf16[2,8,4,256]{3,2,1,0:T(4,128)(2,1)S(1)}, bf16[2,8,4,256]{3,2,1,0:T(4,128)(2,1)S(1)}, u32[]{:S(2)}, u32[]{:S(2)}) %collective-permute-start.11) | collective-permute-done | bytes 32800 | tf_op jit(solution)/shard_map/ppermute | solution.py:39
  (78 shorter events, 48.1 us)
Async XLA Ops:
  6.5 50.8 %copy-start = (bf16[3,3,3,32,512]{4,3,2,1,0:T(8,128)(2,1)S(1)}, bf16[3,3,3,32,512]{4,3,2,1,0:T(8,128)(2,1)}, u32[]{:S(2)}) copy-start(bf16[3,3,3,32,512]{4,3,2,1,0:T(8,128)(2,1)} %param.9) | copy-start | bytes 2654212
  6.5 192.5 %reduce-scatter.2.cloned.1.call-start = ((), (), s32[]{:S(2)}) async-start(), calls=%async_computation.1 | async-start | bytes 1179648 | tf_op jit(solution)/shard_map/reduce_scatter | solution.py:133
  6.5 41.1 %collective-permute-start.3 = (bf16[3,3,3,32,512]{4,3,2,1,0:T(8,128)(2,1)}, bf16[3,3,3,32,512]{4,3,2,1,0:T(8,128)(2,1)}, u32[]{:S(2)}, u32[]{:S(2)}) collective-permute-start(bf16[3,3,3,32,512]{4,3,2,1,0:T(8,128)(2,1)} %param.9), channel_id=1, source_target_pairs={{0,2},{2,4},{4,6},{6,8},{8,10},{10,12},{12,14},{14,0},{1,3},{3,5},... | collective-permute-start | bytes 2654216 | tf_op jit(solution)/shard_map/ppermute | solution.py:19
  9.5 65.4 %collective-permute-start.4 = (bf16[3,3,3,32,512]{4,3,2,1,0:T(8,128)(2,1)}, bf16[3,3,3,32,512]{4,3,2,1,0:T(8,128)(2,1)}, u32[]{:S(2)}, u32[]{:S(2)}) collective-permute-start(bf16[3,3,3,32,512]{4,3,2,1,0:T(8,128)(2,1)} %param.9), channel_id=1, source_target_pairs={{0,14},{2,0},{4,2},{6,4},{8,6},{10,8},{12,10},{14,12},{1,15},{3,1}... | collective-permute-start | bytes 2654216 | tf_op jit(solution)/shard_map/ppermute | solution.py:24
  13.4 36.7 %collective-permute-start = (bf16[2,8,4,256]{3,2,1,0:T(4,128)(2,1)S(1)}, bf16[2,8,4,256]{3,2,1,0:T(4,128)(2,1)S(1)}, u32[]{:S(2)}, u32[]{:S(2)}) collective-permute-start(bf16[2,8,4,256]{3,2,1,0:T(4,128)(2,1)S(1)} %get-tuple-element.40), channel_id=1, source_target_pairs={{0,4},{4,8},{8,12},{1,5},{5,9},{9,13},{2,6},{6,10},{10,14},{3,7},{... | collective-permute-start | bytes 98312 | tf_op jit(solution)/shard_map/ppermute | solution.py:38
  15.3 34.8 %collective-permute-start.1 = (bf16[2,8,4,256]{3,2,1,0:T(4,128)(2,1)S(1)}, bf16[2,8,4,256]{3,2,1,0:T(4,128)(2,1)S(1)}, u32[]{:S(2)}, u32[]{:S(2)}) collective-permute-start(bf16[2,8,4,256]{3,2,1,0:T(4,128)(2,1)S(1)} %get-tuple-element.41), channel_id=1, source_target_pairs={{4,0},{8,4},{12,8},{5,1},{9,5},{13,9},{6,2},{10,6},{14,10},{7,3},{... | collective-permute-start | bytes 98312 | tf_op jit(solution)/shard_map/ppermute | solution.py:39
  47.7 32.7 %collective-permute-start.5 = (bf16[3,3,3,32,512]{4,3,2,1,0:T(8,128)(2,1)}, bf16[3,3,3,32,512]{4,3,2,1,0:T(8,128)(2,1)}, u32[]{:S(2)}, u32[]{:S(2)}) collective-permute-start(bf16[3,3,3,32,512]{4,3,2,1,0:T(8,128)(2,1)} %collective-permute-done.3), channel_id=1, source_target_pairs={{0,2},{2,4},{4,6},{6,8},{8,10},{10,12},{12,14},{14,0},{1,3},{3,5},... | collective-permute-start | bytes 2654216 | tf_op jit(solution)/shard_map/ppermute | solution.py:19
  51.1 21.5 %collective-permute-start.2 = (bf16[2,8,24,256]{3,2,1,0:T(8,128)(2,1)S(1)}, bf16[2,8,24,256]{3,2,1,0:T(8,128)(2,1)S(1)}, u32[]{:S(2)}, u32[]{:S(2)}) collective-permute-start(bf16[2,8,24,256]{3,2,1,0:T(8,128)(2,1)S(1)} %pad_maximum_fusion.1), channel_id=1, source_target_pairs={{0,2},{1,3},{4,6},{5,7},{8,10},{9,11},{12,14},{13,15},{16,18},{17,... | collective-permute-start | bytes 589832 | tf_op jit(solution)/shard_map/ppermute | solution.py:47
  57.3 25.2 %copy-start.1 = (bf16[2,8,16,256]{3,2,1,0:T(8,128)(2,1)S(1)}, bf16[2,8,16,256]{3,2,1,0:T(8,128)(2,1)}, u32[]{:S(2)}) copy-start(bf16[2,8,16,256]{3,2,1,0:T(8,128)(2,1)} %param.6) | copy-start | bytes 393220
  57.3 25.2 %copy-start.3 = (f32[256]{0:T(256)S(1)}, f32[256]{0:T(256)}, u32[]{:S(2)}) copy-start(f32[256]{0:T(256)} %param.8) | copy-start | bytes 3076
  57.3 25.2 %copy-start.4 = (f32[256]{0:T(256)S(1)}, f32[256]{0:T(256)}, u32[]{:S(2)}) copy-start(f32[256]{0:T(256)} %param.7) | copy-start | bytes 3076
  74.9 39.6 %collective-permute-start.6 = (bf16[3,3,3,32,512]{4,3,2,1,0:T(8,128)(2,1)}, bf16[3,3,3,32,512]{4,3,2,1,0:T(8,128)(2,1)}, u32[]{:S(2)}, u32[]{:S(2)}) collective-permute-start(bf16[3,3,3,32,512]{4,3,2,1,0:T(8,128)(2,1)} %collective-permute-done.4), channel_id=1, source_target_pairs={{0,14},{2,0},{4,2},{6,4},{8,6},{10,8},{12,10},{14,12},{1,15},{3,1}... | collective-permute-start | bytes 2654216 | tf_op jit(solution)/shard_map/ppermute | solution.py:24
  80.4 53.2 %collective-permute-start.7 = (bf16[3,3,3,32,512]{4,3,2,1,0:T(8,128)(2,1)}, bf16[3,3,3,32,512]{4,3,2,1,0:T(8,128)(2,1)}, u32[]{:S(2)}, u32[]{:S(2)}) collective-permute-start(bf16[3,3,3,32,512]{4,3,2,1,0:T(8,128)(2,1)} %collective-permute-done.5), channel_id=1, source_target_pairs={{0,2},{2,4},{4,6},{6,8},{8,10},{10,12},{12,14},{14,0},{1,3},{3,5},... | collective-permute-start | bytes 2654216 | tf_op jit(solution)/shard_map/ppermute | solution.py:19
  114.5 33.1 %collective-permute-start.8 = (bf16[3,3,3,32,512]{4,3,2,1,0:T(8,128)(2,1)}, bf16[3,3,3,32,512]{4,3,2,1,0:T(8,128)(2,1)S(1)}, u32[]{:S(2)}, u32[]{:S(2)}) collective-permute-start(bf16[3,3,3,32,512]{4,3,2,1,0:T(8,128)(2,1)} %collective-permute-done.6), channel_id=1, source_target_pairs={{0,14},{2,0},{4,2},{6,4},{8,6},{10,8},{12,10},{14,12},{1,15},{3,1}... | collective-permute-start | bytes 2654216 | tf_op jit(solution)/shard_map/ppermute | solution.py:24
  133.6 24.3 %collective-permute-start.9 = (bf16[3,3,3,32,512]{4,3,2,1,0:T(8,128)(2,1)}, bf16[3,3,3,32,512]{4,3,2,1,0:T(8,128)(2,1)S(1)}, u32[]{:S(2)}, u32[]{:S(2)}) collective-permute-start(bf16[3,3,3,32,512]{4,3,2,1,0:T(8,128)(2,1)} %collective-permute-done.7), channel_id=1, source_target_pairs={{0,2},{2,4},{4,6},{6,8},{8,10},{10,12},{12,14},{14,0},{1,3},{3,5},... | collective-permute-start | bytes 2654216 | tf_op jit(solution)/shard_map/ppermute | solution.py:19
  190.4 3.0 %copy-start.2 = (s32[4]{0:T(128)S(1)}, s32[4]{0:T(128)}, u32[]{:S(2)}) copy-start(s32[4]{0:T(128)} %param.11) | copy-start | bytes 52
  190.4 8.6 %copy-start.5 = (f32[256]{0:T(256)S(1)}, f32[256]{0:T(256)}, u32[]{:S(2)}) copy-start(f32[256]{0:T(256)} %param.10) | copy-start | bytes 3076
  200.2 5.2 %collective-permute-start.10 = (bf16[2,8,4,256]{3,2,1,0:T(4,128)(2,1)S(1)}, bf16[2,8,4,256]{3,2,1,0:T(4,128)(2,1)S(1)}, u32[]{:S(2)}, u32[]{:S(2)}) collective-permute-start(bf16[2,8,4,256]{3,2,1,0:T(4,128)(2,1)S(1)} %get-tuple-element.38), channel_id=1, source_target_pairs={{0,4},{4,8},{8,12},{1,5},{5,9},{9,13},{2,6},{6,10},{10,14},{3,7},{... | collective-permute-start | bytes 98312 | tf_op jit(solution)/shard_map/ppermute | solution.py:38
  203.8 5.8 %collective-permute-start.11 = (bf16[2,8,4,256]{3,2,1,0:T(4,128)(2,1)S(1)}, bf16[2,8,4,256]{3,2,1,0:T(4,128)(2,1)S(1)}, u32[]{:S(2)}, u32[]{:S(2)}) collective-permute-start(bf16[2,8,4,256]{3,2,1,0:T(4,128)(2,1)S(1)} %get-tuple-element.39), channel_id=1, source_target_pairs={{4,0},{8,4},{12,8},{5,1},{9,5},{13,9},{6,2},{10,6},{14,10},{7,3},{... | collective-permute-start | bytes 98312 | tf_op jit(solution)/shard_map/ppermute | solution.py:39
Sparse Core Ops, SparseCore 0:
  193.5 5.5 reduce-scatter.1
